TPU v7x, 256 devices: a whole 4x4x8 slice. The times are simulated.
256 devices in a mesh: rows: 64 (over z, y, core), cols: 4 (over x).
Axes of the slice: x: 4, y: 4, z: 8, core: 2. Of those that a mesh axis runs over, the one named last changes fastest.
Arguments:
- feats_t: bfloat16 [128, 131072], P('cols', 'rows'), may hold values from -6 to 6
- adj_index: int32 [1024, 16], replicated, may hold values from 0 to 1023, as said below
- adj_weight: bfloat16 [1024, 16, 128, 128], P('rows'), as said below
- weight: bfloat16 [128, 256], replicated, may hold values from -0.5 to 0.5
- cotangent_t: bfloat16 [256, 131072], P('cols', 'rows'), may hold values from -6 to 6
Outputs:
- output_t: bfloat16 [256, 131072], P('cols', 'rows')
- weight_grad: float32 [128, 256], P('cols')
- feat_grad: float32 [128, 131072], P('cols', 'rows')
Inputs may be any that keep to these rules, and one draw needn't show every extreme that they name: `adj_index`: slot 0 of row block i names block i itself. Blocks are grouped 16 to a device in order. Slot 1 names a block of the next device (device index plus one, cyclically). The row blocks of one device name at most 4 distinct blocks of any other device, and exactly 4 of the next one. A block may stand in several slots of one row block. `adj_weight`: Nonnegative; about one entry in eight is nonzero.
All inputs are finite; a program needn't handle non-finite values.
Results may differ from a plain program's by a relative error of at most 0.0054.
Values may be sent and summed in bfloat16 or wider, within the bound.
A program may use at most 128 MiB of HBM per device.

v0:
```python
import math

import jax
import jax.numpy as jnp
from jax import lax
from jax.sharding import PartitionSpec as P


def body(feats_t, adj_index, adj_weight, weight, cotangent_t):
    feat_rows, node_cols = feats_t.shape
    blocks_n = adj_weight.shape[0]
    slots_n = adj_weight.shape[1]
    tile_n = adj_weight.shape[2]
    row_devs = lax.axis_size("rows")
    row_pos = lax.axis_index("rows")
    col_pos = lax.axis_index("cols")
    unit_rows = cotangent_t.shape[0]
    own_index = lax.dynamic_slice_in_dim(adj_index, row_pos * blocks_n, blocks_n, 0)
    own_flat = own_index.reshape(-1)
    local_tiles = feats_t.reshape(feat_rows, blocks_n, tile_n).transpose(1, 0, 2)
    whole_panel = lax.all_gather(local_tiles, "rows", axis=0, tiled=True)
    picked = whole_panel[own_index]
    aggregate = jnp.einsum("bkfj,bkij->fbi", picked, adj_weight, preferred_element_type=jnp.float32)
    aggregated = aggregate.reshape(feat_rows, node_cols).astype(jnp.bfloat16)
    w_slab = lax.dynamic_slice_in_dim(weight, col_pos * unit_rows, unit_rows, 1)
    pre_act = lax.dot_general(
        w_slab,
        lax.all_gather(aggregated, "cols", axis=0, tiled=True),
        (((0,), (0,)), ((), ())),
        preferred_element_type=jnp.float32,
    )
    output_t = jax.nn.silu(pre_act).astype(jnp.bfloat16)
    sigm = jax.nn.sigmoid(pre_act)
    pre_grad = (cotangent_t.astype(jnp.float32) * sigm * (1.0 + pre_act * (1.0 - sigm))).astype(
        jnp.bfloat16
    )
    w_mine = lax.dynamic_slice_in_dim(weight, col_pos * feat_rows, feat_rows, 0)
    portion = lax.all_gather(pre_grad, "cols", axis=0, tiled=True)
    grad_acc = jnp.dot(w_mine, portion, preferred_element_type=jnp.float32)
    block_grad = lax.dot_general(
        aggregated, portion, (((1,), (1,)), ((), ())), preferred_element_type=jnp.float32
    )
    grad_scale = 1.0 / math.sqrt(node_cols * row_devs)
    weight_grad = lax.psum(block_grad, "rows") * grad_scale
    agg_grad = grad_acc.astype(jnp.bfloat16)
    contrib = jnp.einsum(
        "fbi,bkij->bkfj",
        agg_grad.reshape(feat_rows, blocks_n, tile_n),
        adj_weight,
        preferred_element_type=jnp.float32,
    )
    contrib_flat = contrib.reshape(blocks_n * slots_n, feat_rows * tile_n)
    buffer = jax.ops.segment_sum(contrib_flat, own_flat, num_segments=row_devs * blocks_n)
    buffer = buffer.reshape(row_devs * blocks_n, feat_rows, tile_n)
    summed = lax.psum_scatter(buffer, "rows", scatter_dimension=0, tiled=True)
    feat_grad = summed.transpose(1, 0, 2).reshape(feat_rows, node_cols)
    return (output_t, weight_grad, feat_grad)


def solution(mesh):
    return jax.shard_map(
        body,
        mesh=mesh,
        in_specs=(P("cols", "rows"), P(), P("rows", None, None, None), P(), P("cols", "rows")),
        out_specs=(P("cols", "rows"), P("cols", None), P("cols", "rows")),
        check_vma=False,
    )
```

profile of v0, /device:TPU:8, one launch (start us, length us, event | category | flops | bytes accessed | tf_op | source)
XLA Modules:
  0.0 464.3 jit_solution(11323263088289372892)
XLA Ops:
  7.2 0.0 copy-start
  7.2 0.0 copy-start.3
  7.2 0.0 all-gather.3.cloned.1.call-start
  7.2 1.0 copy.36
  8.2 0.7 copy.22
  8.9 0.0 all-gather.3.cloned.1.call-update
  8.9 0.0 all-gather.5.cloned.1.call-start
  9.0 0.8 compare_select_fusion
  9.8 0.1 copy.23
  9.8 0.1 reshape.30
  9.9 86.1 %all-gather.3.cloned.1.call-done = bf16[1024,32,128]{2,1,0:T(8,128)(2,1)} async-done(((bf16[16,32,128]{2,1,0:T(8,128)(2,1)}), bf16[1024,32,128]{2,1,0:T(8,128)(2,1)}) %all-gather.3.cloned.1.call-update) | async-done | bytes 8388624 | tf_op jit(solution)/shard_map/all_gather | solution.py:21
  96.0 4.4 gather_fusion
  100.4 6.2 %fusion.5 = bf16[16,4,8,128]{3,2,1,0:T(8,128)(2,1)S(1)} fusion(bf16[16,16,32,128]{3,2,1,0:T(8,128)(2,1)S(1)} %bitcast.45, bf16[16,16,128,128]{3,2,1,0:T(8,128)(2,1)} %param.7), kind=kOutput, calls=%fused_computation.9 | convolution fusion | flops 268500992 | bytes 10616832 | tf_op jit(solution)/shard_map/bkfj,bkij->fbi/dot_general | solution.py:23
  106.6 13.1 %all_gather.10 = bf16[128,2048]{1,0:T(8,128)(2,1)S(1)} all-gather(bf16[32,2048]{1,0:T(8,128)(2,1)S(1)} %bitcast.47), channel_id=1, replica_groups=mesh['rows'=64,'cols'=4] {'cols'}, dimensions={0}, use_global_device_ids=true | all-gather | bytes 655360 | tf_op jit(solution)/shard_map/all_gather | solution.py:28
  119.7 0.0 copy-done
  119.7 0.0 copy-done.3
  119.7 1.3 multiply_convert_fusion
  121.0 0.0 all-gather.5.cloned.1.call-update
  121.1 0.2 reduce-scatter.2.cloned.1.call-start
  121.3 0.1 copy.25
  121.4 0.1 reshape.38
  121.5 24.9 %all-gather.5.cloned.1.call-done = bf16[256,2048]{1,0:T(8,128)(2,1)} async-done(((bf16[64,2048]{1,0:T(8,128)(2,1)}), bf16[256,2048]{1,0:T(8,128)(2,1)}) %all-gather.5.cloned.1.call-update) | async-done | bytes 1048592 | tf_op jit(solution)/shard_map/all_gather | solution.py:38
  146.4 1.5 fusion.6
  147.9 6.5 %fusion.7 = f32[16,32,16,128]{3,1,2,0:T(8,128)} fusion(bf16[16,16,128,128]{3,2,1,0:T(8,128)(2,1)} %param.7, bf16[32,16,128,1]{2,1,0,3:T(8,128)(2,1)S(1)} %bitcast.46), kind=kOutput, calls=%fused_computation.16 | convolution fusion | flops 268435456 | bytes 12713984 | tf_op jit(solution)/shard_map/fbi,bkij->bkfj/dot_general | solution.py:46
  154.5 16.7 %scatter_custom_fusion = f32[1024,4096]{1,0:T(8,128)} fusion(s32[256]{0:T(256)S(1)} %reshape.38, f32[]{:T(128)} %constant.11.clone.1, f32[32,8,32,128]{3,2,1,0:T(8,128)} %bitcast.44), kind=kCustom, calls=%fused_computation.2 | custom fusion | flops 1048576 | bytes 20971524 | tf_op jit(solution)/shard_map/scatter-add | solution.py:53
  171.2 17.5 %copy.27 = f32[1024,4096]{0,1:T(8,128)} copy(f32[1024,4096]{1,0:T(8,128)} %scatter_custom_fusion) | data formatting | bytes 33554432 | tf_op jit(solution)/shard_map/scatter-add | solution.py:53
  188.6 17.4 %copy.28 = f32[1024,32,128]{2,1,0:T(8,128)} copy(f32[1024,32,128]{0,2,1:T(8,128)} %bitcast.43) | data formatting | bytes 33554432 | tf_op jit(solution)/shard_map/reshape | solution.py:54
  206.0 0.0 copy-start.1
  206.0 0.0 copy-start.2
  206.0 0.0 reduce-scatter.2.cloned.1.call-update
  206.0 1.2 copy-done.2
  207.3 0.4 fusion.14
  207.7 247.8 %psum.7 = f32[32,256]{1,0:T(8,128)S(1)} all-reduce(f32[32,256]{1,0:T(8,128)S(1)} %fusion.14), channel_id=1, replica_groups=mesh['rows'=64,'cols'=4] {'rows'}, use_global_device_ids=true, to_apply=%region_0.1 | all-reduce | flops 8192 | bytes 65536 | tf_op jit(solution)/shard_map/psum | solution.py:44
  455.5 0.6 broadcast_multiply_fusion
  456.1 0.0 reduce-scatter.2.cloned.1.call-done
  456.1 1.7 copy_bitcast_fusion
  457.8 0.0 copy-done.1
  (3 shorter events, 0.1 us)
Async XLA Ops:
  7.2 112.6 %copy-start = (bf16[128,256]{1,0:T(8,128)(2,1)S(1)}, bf16[128,256]{1,0:T(8,128)(2,1)}, u32[]{:S(2)}) copy-start(bf16[128,256]{1,0:T(8,128)(2,1)} %param.8) | copy-start | bytes 196612
  7.2 112.6 %copy-start.3 = (bf16[64,2048]{1,0:T(8,128)(2,1)S(1)}, bf16[64,2048]{1,0:T(8,128)(2,1)}, u32[]{:S(2)}) copy-start(bf16[64,2048]{1,0:T(8,128)(2,1)} %param.9) | copy-start | bytes 786436
  7.2 88.9 %all-gather.3.cloned.1.call-start = ((), (), s32[]{:S(2)}) async-start(), calls=%async_computation.1 | async-start | bytes 8519680 | tf_op jit(solution)/shard_map/all_gather | solution.py:21
  8.9 137.5 %all-gather.5.cloned.1.call-start = ((), (), s32[]{:S(2)}) async-start(), calls=%async_computation.2 | async-start | bytes 1310720 | tf_op jit(solution)/shard_map/all_gather | solution.py:38
  121.1 335.1 %reduce-scatter.2.cloned.1.call-start = ((), (), s32[]{:S(2)}) async-start(), calls=%async_computation.3 | async-start | bytes 17039360 | tf_op jit(solution)/shard_map/reduce_scatter | solution.py:55
  206.0 251.8 %copy-start.1 = (bf16[128,256]{1,0:T(8,128)(2,1)S(1)}, bf16[128,256]{1,0:T(8,128)(2,1)}, u32[]{:S(2)}) copy-start(bf16[128,256]{1,0:T(8,128)(2,1)} %param.8) | copy-start | bytes 196612
  206.0 1.3 copy-start.2
Sparse Core Ops, SparseCore 0:
  11.4 84.6 all-gather.2
  121.2 25.1 all-gather.4
  206.2 189.3 reduce-scatter.1
where the time goes:
time: 469 us; the launch traced here: 464 us
  blocking collectives  261 us (56%)
  waiting for transfers between devices  111 us (24%)
  local copies, waits for them, and re-layouts  44.2 us (9%)
  other arithmetic  18.1 us (4%)
  matrix products  15.9 us (3%)
  between operations  13.8 us (3%)
    psum x1, blocking collectives, body(): weight_grad = lax.psum(block_grad, 'rows') * grad_scale  248 us
    all_gather x1, waiting for transfers between devices, body(): whole_panel = lax.all_gather(local_tiles, 'rows', axis=0, tiled=True)  86.1 us
    all_gather x1, waiting for transfers between devices, body(): portion = lax.all_gather(pre_grad, 'cols', axis=0, tiled=True)  24.9 us
    scatter-add x1, local copies, waits for them, and re-layouts, body(): jax.ops.segment_sum(contrib_flat, own_flat, num_segments=row_devs * block...  17.5 us
    reshape x1, local copies, waits for them, and re-layouts, body(): buffer = buffer.reshape(row_devs * blocks_n, feat_rows, tile_n)  17.4 us
    scatter-add x1, other arithmetic, body(): jax.ops.segment_sum(contrib_flat, own_flat, num_segments=row_devs * block...  16.7 us
    all_gather x1, blocking collectives, body(): lax.all_gather(aggregated, 'cols', axis=0, tiled=True)  13.1 us
  transfers between devices with their start and end apart: 3, of which 2 were waited for; matrix products, arithmetic and copies ran while one was open for 0% of the time, Pallas kernels for 0%

commit v1 on v0

v1 whole, which is shorter than its diff:
```python
import math

import jax
import jax.numpy as jnp
from jax import lax
from jax.experimental import pallas as pl
from jax.experimental.pallas import tpu as pltpu
from jax.sharding import PartitionSpec as P

MESH = pl.DeviceIdType.MESH
NZ, NY, NC, NX = 8, 4, 2, 4
BLK, KB, TILE, CAP, FR, UR = 16, 16, 128, 4, 32, 64
NODES_DEV = BLK * TILE
CH = 4
CN = NODES_DEV // CH
OWN = 64 * CAP
ZERO = BLK * KB
FWD_ORDER = (0, 7, 1, 6, 2, 5, 3, 4)
BWD_ORDER = (4, 3, 5, 2, 6, 1, 7, 0)
F32, BF16 = jnp.float32, jnp.bfloat16
NT = (((1,), (1,)), ((), ()))


def tables(adj_index, r, z, y, c):
    i32 = jnp.int32
    rows8 = lax.dynamic_slice_in_dim(adj_index, z * 8 * BLK, 8 * BLK, 0).reshape(8, 1, BLK * KB)
    t = jnp.arange(NZ * BLK, dtype=i32)
    target = (t // BLK) * (8 * BLK) + y * (2 * BLK) + c * BLK + t % BLK
    named = jnp.any(rows8 == target[None, :, None], axis=2)
    named = named.reshape(8, NZ, BLK)
    b = jnp.arange(BLK, dtype=i32)
    rank = jnp.sum(jnp.where((b[None, :] < b[:, None])[None, None], named[:, :, None, :], False), axis=3, dtype=i32)
    k = jnp.arange(CAP, dtype=i32)
    hit = named[:, :, None, :] & (rank[:, :, None, :] == k[None, None, :, None])
    send = jnp.sum(jnp.where(hit, b[None, None, None, :], 0), axis=3, dtype=i32)
    d = jnp.arange(8, dtype=i32)
    own_pair = (d[:, None, None] == y * 2 + c) & (jnp.arange(NZ, dtype=i32)[None, :, None] == z)
    take = jnp.where(named & ~own_pair, d[:, None, None] * CAP + jnp.minimum(rank, CAP - 1), 8 * CAP)
    take = take.transpose(1, 2, 0)
    own = lax.dynamic_slice_in_dim(adj_index, r * BLK, BLK, 0).reshape(BLK * KB)
    j = jnp.arange(64 * BLK, dtype=i32)
    present = jnp.any(own[None, :] == j[:, None], axis=1)
    before = present[None, :] & (j[None, :] // BLK == own[:, None] // BLK) & (j[None, :] < own[:, None])
    slot = (own // BLK) * CAP + jnp.sum(before, axis=1, dtype=i32)
    slot = jnp.where(own // BLK == r, OWN + own % BLK, slot)
    e = jnp.arange(BLK * KB, dtype=i32)
    pos = jnp.sum((slot[None, :] < slot[:, None]) | ((slot[None, :] == slot[:, None]) & (e[None, :] < e[:, None])), axis=1, dtype=i32)
    at = pos[None, :] == e[:, None]
    order = jnp.sum(jnp.where(at, e[None, :], 0), axis=1, dtype=i32)
    sslot = jnp.sum(jnp.where(at, slot[None, :], 0), axis=1, dtype=i32)
    keep = jnp.concatenate([jnp.zeros((1,), F32), (sslot[1:] == sslot[:-1]).astype(F32)])
    s = jnp.arange(OWN + BLK, dtype=i32)
    count = jnp.sum(slot[None, :] <= s[:, None], axis=1, dtype=i32)
    less = jnp.sum(slot[None, :] < s[:, None], axis=1, dtype=i32)
    last = jnp.where(count > less, count - 1, ZERO)
    return send.reshape(-1), slot, order, keep, last, take.reshape(-1)


def kernel(
    send_t, slot_t, order_t, keep_t, last_t, take_t, feats, cot, w_rows, w_cols, adj_hbm,
    out, wg_out, fg_out,
    adj, zb, pk, panel, fwp, fwm, xg, gsend, grecv, gown, grad, pref, pk2, rb, fw2p, fw2m, zs_buf, zrp, zrm,
    wpart, wsib, wy, wz, wx, wt,
    adj_sem, zss, zrs, yss, yrs, xss, xrs, gss, grs, yss2, yrs2, zss2, zrs2, wss, wrs,
):
    r = lax.axis_index("rows")
    x = lax.axis_index("cols")
    z, y, c = r // 8, (r // 2) % 4, r % 2
    me = y * 2 + c

    def dev(dz=0, dy=0, dc=0, dx=0):
        row = ((z + dz) % NZ) * 8 + ((y + dy) % NY) * 2 + (c + dc) % 2
        return {"rows": row, "cols": (x + dx) % NX}

    def rcopy(src, dst, ss, rs, **off):
        return pltpu.make_async_remote_copy(
            src_ref=src, dst_ref=dst, send_sem=ss, recv_sem=rs, device_id=dev(**off), device_id_type=MESH
        )

    adj_copy = pltpu.make_async_copy(adj_hbm, adj, adj_sem)
    adj_copy.start()
    peers = [dict(dz=d) for d in range(1, 8)]
    peers += [dict(dy=a, dc=b) for a in range(4) for b in range(2) if (a or b) and (a, b) != (2, 1)]
    peers += [dict(dx=a, dc=b) for a in range(1, 4) for b in range(2)]
    barrier = pltpu.get_barrier_semaphore()
    for off in peers:
        pl.semaphore_signal(barrier, inc=1, device_id=dev(**off), device_id_type=MESH)

    for b in range(BLK):
        blk = feats[:, b * TILE:(b + 1) * TILE]
        zb[0][b] = blk
        panel[OWN + b] = blk
    pl.semaphore_wait(barrier, len(peers))

    pending = []

    half = BLK // 2
    whole = pl.ds(0, BLK)
    zcopies = {}

    def zsend(src, dst, direction, blocks):
        cp = rcopy(zb[src].at[blocks], zb[dst].at[blocks], zss.at[dst + 8 * (direction > 0)], zrs.at[dst + 8 * (direction > 0)], dz=direction)
        cp.start()
        zcopies.setdefault(dst, []).append(cp)
        pending.append(cp)

    def pack(dz, src, put, self_put):
        zs = (z + dz) % NZ

        def one(i, carry):
            dd = ((y + i // 2) % NY) * 2 + (c + i % 2) % 2
            src(i, dd, zs)
            return carry

        lax.fori_loop(0 if self_put else 1, 8, one, 0)

    def ysends(dz, packs, dst_of, fp, fm, ss, rs, copies):
        list_ = []
        for n, (dy, dc) in enumerate(((1, 0), (1, 1), (3, 0), (3, 1), (0, 1))):
            cp = rcopy(packs.at[dz, dy * 2 + dc], dst_of(dz, y), ss.at[dz * 9 + n], rs.at[dz * 9 + n], dy=dy, dc=dc)
            list_.append(cp)
        a = rcopy(packs.at[dz, 4], fp.at[dz], ss.at[dz * 9 + 7], rs.at[dz * 9 + 7], dy=1)
        b = rcopy(packs.at[dz, 5], fm.at[dz], ss.at[dz * 9 + 8], rs.at[dz * 9 + 8], dy=3)
        for cp in (a, b, *list_):
            cp.start()
            pending.append(cp)
        copies[dz] = (list_, a, b)

    def forwards(dz, dst_of, fp, fm, ss, rs, copies):
        list_, a, b = copies[dz]
        a.wait_recv()
        f = rcopy(fp.at[dz], dst_of(dz, (y + 3) % NY), ss.at[dz * 9 + 5], rs.at[dz * 9 + 5], dy=1, dc=0)
        f.start()
        b.wait_recv()
        g = rcopy(fm.at[dz], dst_of(dz, (y + 1) % NY), ss.at[dz * 9 + 6], rs.at[dz * 9 + 6], dy=3, dc=1)
        g.start()
        pending.extend((f, g))
        list_ += [f, g]

    def panel_of(dz, yy):
        return panel.at[pl.ds((((z + dz) % NZ) * 8 + yy * 2 + c) * CAP, CAP)]

    ycopies = {}
    zsend(0, 7, 1, whole)
    zsend(0, 1, -1, whole)
    previous = None
    for dz in FWD_ORDER:
        if dz:
            for cp in zcopies[dz]:
                cp.wait_recv()
            if dz in (7, 6):
                zsend(dz, dz - 1, 1, whole)
            elif dz == 5:
                zsend(5, 4, 1, pl.ds(0, half))
            elif dz in (1, 2):
                zsend(dz, dz + 1, -1, whole)
            elif dz == 3:
                zsend(3, 4, -1, pl.ds(half, half))

        def message(i, dd, zs, dz=dz):
            for k in range(CAP):
                pk[dz, i, k] = zb[dz][send_t[(dd * NZ + zs) * CAP + k]]

        pack(dz, message, None, False)
        if dz:
            zs = (z + dz) % NZ
            for k in range(CAP):
                panel[(zs * 8 + me) * CAP + k] = zb[dz][send_t[(me * NZ + zs) * CAP + k]]
        ysends(dz, pk, panel_of, fwp, fwm, yss, yrs, ycopies)
        if previous is not None:
            forwards(previous, panel_of, fwp, fwm, yss, yrs, ycopies)
        previous = dz
    forwards(previous, panel_of, fwp, fwm, yss, yrs, ycopies)
    adj_copy.wait()
    for dz in FWD_ORDER:
        for cp in ycopies[dz][0]:
            cp.wait_recv()

    xcopies = {}
    for q in range(CH):

        def block(n, carry, q=q):
            i = q * (BLK // CH) + n
            acc = jnp.zeros((FR, TILE), F32)
            for k in range(0, KB, 2):
                left = jnp.concatenate([panel[slot_t[i * KB + k]], panel[slot_t[i * KB + k + 1]]], axis=1)
                right = jnp.concatenate([adj[i * KB + k], adj[i * KB + k + 1]], axis=1)
                acc += lax.dot_general(left, right, NT, preferred_element_type=F32)
            xg[0, q, :, pl.ds(pl.multiple_of(n * TILE, TILE), TILE)] = acc.astype(BF16)
            return carry

        lax.fori_loop(0, BLK // CH, block, 0)
        for dx in (2, 1, 3):
            cp = rcopy(xg.at[0, q], xg.at[4 - dx, q], xss.at[q * 4 + dx], xrs.at[q * 4 + dx], dx=dx)
            cp.start()
            pending.append(cp)
            xcopies[q, dx] = cp

    gcopies = {}
    for q in range(CH):
        cols = pl.ds(q * CN, CN)
        for dx in (1, 3, 2):
            xcopies[q, dx].wait_recv()
        agg = xg[:, q].reshape(NX * FR, CN)
        pre = jnp.dot(w_cols[...], agg, preferred_element_type=F32)
        sig = jax.nn.sigmoid(pre)
        out[:, cols] = (pre * sig).astype(BF16)
        pg = (cot[:, cols].astype(F32) * sig * (1.0 + pre * (1.0 - sig))).astype(BF16)
        part = jnp.dot(w_rows[...], pg, preferred_element_type=F32)
        gown[q] = part[0:FR]
        for dx in (2, 1, 3):
            gsend[dx, q] = part[dx * FR:(dx + 1) * FR].astype(BF16)
            cp = rcopy(gsend.at[dx, q], grecv.at[4 - dx, q], gss.at[q * 4 + dx], grs.at[q * 4 + dx], dx=dx)
            cp.start()
            pending.append(cp)
            gcopies[q, dx] = cp
        wg = lax.dot_general(pg, agg, NT, preferred_element_type=F32)
        if q == 0:
            wpart[...] = wg
        else:
            wpart[...] += wg

    hu = UR // 2
    w1 = rcopy(wpart.at[pl.ds(pl.multiple_of((1 - c) * hu, 8), hu)], wsib, wss.at[0], wrs.at[0], dc=1)
    w1.start()
    pending.append(w1)

    for q in range(CH):
        for dx in (1, 3, 2):
            gcopies[q, dx].wait_recv()
        g = gown[q] + grecv[1, q].astype(F32) + grecv[2, q].astype(F32) + grecv[3, q].astype(F32)
        g = g.astype(BF16)
        for n in range(BLK // CH):
            grad[q * (BLK // CH) + n] = g[:, n * TILE:(n + 1) * TILE]

    w1.wait_recv()
    wy[y] = wpart[pl.ds(pl.multiple_of(c * hu, 8), hu)] + wsib[...]
    w2 = []
    for dy in (1, 2, 3):
        cp = rcopy(wy.at[y], wy.at[y], wss.at[dy], wrs.at[dy], dy=dy)
        cp.start()
        pending.append(cp)
        w2.append(cp)

    def entry(p, carry):
        e = order_t[p]
        pref[p] = jnp.dot(grad[lax.shift_right_logical(e, 4)], adj[e], preferred_element_type=F32)
        return carry

    lax.fori_loop(0, BLK * KB, entry, 0, unroll=8)

    def running(p, acc):
        acc = pref[p] + keep_t[p] * acc
        pref[p] = acc
        return acc

    lax.fori_loop(0, BLK * KB, running, jnp.zeros((FR, TILE), F32), unroll=8)
    pref[ZERO] = jnp.zeros((FR, TILE), F32)

    for cp in w2:
        cp.wait_recv()
    wz[z] = (wy[0] + wy[1]) + (wy[2] + wy[3])
    w3 = []
    for dz in range(1, NZ):
        cp = rcopy(wz.at[z], wz.at[z], wss.at[3 + dz], wrs.at[3 + dz], dz=dz)
        cp.start()
        pending.append(cp)
        w3.append(cp)

    ycopies2 = {}

    def rb_of(dz, yy):
        return rb[dz].at[pl.ds((yy * 2 + c) * CAP, CAP)]

    for dz in range(NZ):
        rb[dz][8 * CAP] = jnp.zeros((FR, TILE), BF16)
    previous = None
    for dz in BWD_ORDER:

        def term(i, dd, zs, dz=dz):
            for k in range(CAP):
                pk2[dz, i, k] = pref[last_t[(zs * 8 + dd) * CAP + k]].astype(BF16)

        pack(dz, term, None, False)
        zs = (z + dz) % NZ
        for k in range(CAP):
            if dz:
                rb[dz][me * CAP + k] = pref[last_t[(zs * 8 + me) * CAP + k]].astype(BF16)
            else:
                rb[dz][me * CAP + k] = jnp.zeros((FR, TILE), BF16)
        ysends(dz, pk2, rb_of, fw2p, fw2m, yss2, yrs2, ycopies2)
        if previous is not None:
            forwards(previous, rb_of, fw2p, fw2m, yss2, yrs2, ycopies2)
        previous = dz
    forwards(previous, rb_of, fw2p, fw2m, yss2, yrs2, ycopies2)

    for cp in w3:
        cp.wait_recv()
    wx[0, c] = (((wz[0] + wz[1]) + (wz[2] + wz[3])) + ((wz[4] + wz[5]) + (wz[6] + wz[7]))) * (
        1.0 / math.sqrt(NODES_DEV * 64)
    )
    w4 = []
    for dx in range(4):
        for dc in range(2):
            if dx or dc:
                n = 11 + dx * 2 + dc
                cp = rcopy(wx.at[0, c], wx.at[(4 - dx) % 4, c], wss.at[n], wrs.at[n], dx=dx, dc=dc)
                cp.start()
                pending.append(cp)
                w4.append(cp)

    zin = {}
    for dz in BWD_ORDER:
        for cp in ycopies2[dz][0]:
            cp.wait_recv()
        for cp in zin.get(dz, ()):
            cp.wait_recv()
        zs = (z + dz) % NZ

        def total(b, carry, dz=dz, zs=zs):
            acc = jnp.zeros((FR, TILE), F32)
            for n in range(8):
                acc += rb[dz][take_t[(zs * BLK + b) * 8 + n]].astype(F32)
            if dz in (1, 2):
                acc += zrp[dz, b].astype(F32)
            if dz in (6, 7):
                acc += zrm[dz, b].astype(F32)
            if dz == 0:
                acc += zrp[0, b].astype(F32) + zrm[0, b].astype(F32) + pref[last_t[OWN + b]]
                fg_out[:, pl.ds(pl.multiple_of(b * TILE, TILE), TILE)] = acc
            else:
                zs_buf[dz, b] = acc.astype(BF16)
            return carry

        def total_more(b, carry, dz=dz, zs=zs):
            off = 0 if dz == 3 else half
            acc = (zrp if dz == 3 else zrm)[dz, off + b].astype(F32)
            for n in range(8):
                acc += rb[dz][take_t[(zs * BLK + off + b) * 8 + n]].astype(F32)
            zs_buf[dz, off + b] = acc.astype(BF16)
            return carry

        def total_less(b, carry, dz=dz, zs=zs):
            off = half if dz == 3 else 0
            acc = jnp.zeros((FR, TILE), F32)
            for n in range(8):
                acc += rb[dz][take_t[(zs * BLK + off + b) * 8 + n]].astype(F32)
            zs_buf[dz, off + b] = acc.astype(BF16)
            return carry

        if dz in (3, 5):
            lax.fori_loop(0, half, total_more, 0)
            lax.fori_loop(0, half, total_less, 0)
        else:
            lax.fori_loop(0, BLK, total, 0)

        def ring(direction, blocks):
            to = dz - direction if dz - direction != 8 else 0
            buf = zrp if direction > 0 else zrm
            n = dz + 8 * (direction > 0)
            cp = rcopy(zs_buf.at[dz, blocks], buf.at[to, blocks], zss2.at[n], zrs2.at[n], dz=direction)
            cp.start()
            pending.append(cp)
            zin.setdefault(to, []).append(cp)

        if dz == 4:
            ring(1, pl.ds(0, half))
            ring(-1, pl.ds(half, half))
        elif dz in (1, 2, 3):
            ring(1, whole)
        elif dz in (5, 6, 7):
            ring(-1, whole)

    for cp in w4:
        cp.wait_recv()
    for dx in range(4):
        for cc in range(2):
            f0 = ((4 - dx) % 4) * FR
            row = pl.multiple_of(((x + dx) % NX) * UR + cc * hu, 8)
            wt[pl.ds(row, hu), 0:FR] = wx[dx, cc][:, f0:f0 + FR]
    wg_out[...] = wt[...].T[0:FR]

    for cp in pending:
        cp.wait_send()


def body(feats_t, adj_index, adj_weight, weight, cotangent_t):
    r = lax.axis_index("rows")
    x = lax.axis_index("cols")
    z, y, c = r // 8, (r // 2) % 4, r % 2
    tabs = tables(adj_index, r, z, y, c)
    w = lax.dynamic_slice_in_dim(weight, x * UR, UR, 1)
    w_rows = lax.dynamic_slice_in_dim(jnp.concatenate([w, w], axis=0), x * FR, NX * FR, 0)
    w_cols = w_rows.T
    vmem = pl.BlockSpec(memory_space=pltpu.VMEM)
    smem = pl.BlockSpec(memory_space=pltpu.SMEM)
    dma = pltpu.SemaphoreType.DMA
    blk = (FR, TILE)
    V = pltpu.VMEM
    return pl.pallas_call(
        kernel,
        out_shape=(
            jax.ShapeDtypeStruct((UR, NODES_DEV), BF16),
            jax.ShapeDtypeStruct((FR, NX * UR), F32),
            jax.ShapeDtypeStruct((FR, NODES_DEV), F32),
        ),
        in_specs=[smem] * 6 + [vmem] * 4 + [pl.BlockSpec(memory_space=pl.ANY)],
        out_specs=(vmem, vmem, vmem),
        scratch_shapes=[
            V((BLK * KB, TILE, TILE), BF16),
            [V((BLK, *blk), BF16) for _ in range(NZ)],
            V((NZ, 8, CAP, *blk), BF16),
            V((OWN + BLK, *blk), BF16),
            V((NZ, CAP, *blk), BF16),
            V((NZ, CAP, *blk), BF16),
            V((NX, CH, FR, CN), BF16),
            V((NX, CH, FR, CN), BF16),
            V((NX, CH, FR, CN), BF16),
            V((CH, FR, CN), F32),
            V((BLK, *blk), BF16),
            V((BLK * KB + 1, *blk), F32),
            V((NZ, 8, CAP, *blk), BF16),
            [V((8 * CAP + 1, *blk), BF16) for _ in range(NZ)],
            V((NZ, CAP, *blk), BF16),
            V((NZ, CAP, *blk), BF16),
            V((NZ, BLK, *blk), BF16),
            V((NZ, BLK, *blk), BF16),
            V((NZ, BLK, *blk), BF16),
            V((UR, NX * FR), F32),
            V((UR // 2, NX * FR), F32),
            V((NY, UR // 2, NX * FR), F32),
            V((NZ, UR // 2, NX * FR), F32),
            V((NX, NC, UR // 2, NX * FR), F32),
            V((NX * UR, TILE), F32),
            dma,
            dma((16,)),
            dma((16,)),
            dma((9 * NZ,)),
            dma((9 * NZ,)),
            dma((16,)),
            dma((16,)),
            dma((16,)),
            dma((16,)),
            dma((9 * NZ,)),
            dma((9 * NZ,)),
            dma((16,)),
            dma((16,)),
            dma((19,)),
            dma((19,)),
        ],
        compiler_params=pltpu.CompilerParams(
            collective_id=0, has_side_effects=True, vmem_limit_bytes=56 * 2**20
        ),
        name="gcn_step",
    )(*tabs, feats_t, cotangent_t, w_rows, w_cols, adj_weight.reshape(BLK * KB, TILE, TILE))


def solution(mesh):
    return jax.shard_map(
        body,
        mesh=mesh,
        in_specs=(P("cols", "rows"), P(), P("rows", None, None, None), P(), P("cols", "rows")),
        out_specs=(P("cols", "rows"), P("cols", None), P("cols", "rows")),
        check_vma=False,
    )
```

time: 469 us -> 123 us (0.26); the launches traced: 464 us -> 123 us
  blocking collectives: 261 us -> 0 us
  waiting for transfers between devices: 111 us -> 0 us
  Pallas kernels: 0 us -> 107 us
  local copies, waits for them, and re-layouts: 44.2 us -> 9.06 us
  matrix products: 15.9 us -> 0 us
  between operations: 13.8 us -> 0.79 us
  other arithmetic: 18.1 us -> 6.2 us
    psum x1 -> x0, blocking collectives: 248 us -> none  [body(): weight_grad = lax.psum(block_grad, 'rows') * grad_scale]
    all_gather x2 -> x0, waiting for transfers between devices: 111 us -> none  [the longest x1 86.1 us: body(): whole_panel = lax.all_gather(local_tiles, 'rows', axis=0, tiled=True)]
    pallas_call x0 -> x1, Pallas kernels: none -> 107 us  [body(): pl.pallas_call(kernel, out_shape=(jax.ShapeDtypeStruct((UR, NODES_DEV), B...]
    reshape x2 -> x3, local copies, waits for them, and re-layouts: 19.1 us -> 1.43 us  [the longest x2 1.34 us: tables(): return (send.reshape(-1), slot, order, keep, last, take.reshape(-1))]
    scatter-add x1 -> x0, local copies, waits for them, and re-layouts: 17.5 us -> none  [body(): jax.ops.segment_sum(contrib_flat, own_flat, num_segments=row_devs * block...]
    scatter-add x1 -> x0, other arithmetic: 16.7 us -> none  [body(): jax.ops.segment_sum(contrib_flat, own_flat, num_segments=row_devs * block...]
    dot_general x5 -> x0, matrix products: 15.9 us -> none  [the longest x1 6.55 us: body(): jnp.einsum('fbi,bkij->bkfj', agg_grad.reshape(feat_rows, blocks_n, tile_n...]
    all_gather x1 -> x0, blocking collectives: 13.1 us -> none  [body(): lax.all_gather(aggregated, 'cols', axis=0, tiled=True)]
  transfers between devices with their start and end apart: 3 -> 0, of which waited for: 2 -> 0; matrix products, arithmetic and copies ran while one was open for 0% -> 0% of each run, Pallas kernels for 0% -> 0%
where the time goes in v1:
time: 123 us
  Pallas kernels  107 us (87%)
  local copies, waits for them, and re-layouts  9.06 us (7%)
  other arithmetic  6.2 us (5%)
    pallas_call x1, Pallas kernels, body(): pl.pallas_call(kernel, out_shape=(jax.ShapeDtypeStruct((UR, NODES_DEV), B...  107 us
    unnamed x8, local copies, waits for them, and re-layouts  4.81 us

profile of v1, /device:TPU:8, one launch (start us, length us, event | category | flops | bytes accessed | tf_op | source)
XLA Modules:
  0.0 123.0 jit_solution(13247010713042935847)
XLA Ops:
  0.6 0.0 copy-start
  0.7 0.1 and_not_fusion
  0.8 0.8 constant_dynamic-slice_fusion.1
  1.6 0.1 copy.19
  1.7 0.1 reshape.300
  1.8 0.2 fusion
  2.0 0.4 convert_reduce_fusion
  2.4 0.0 copy-start.1
  2.5 0.2 convert_reduce_fusion.4
  2.6 0.7 select_reduce_fusion
  3.4 0.1 slice_compare_fusion
  3.5 0.7 add_convert_fusion.keep_t
  4.1 0.2 convert_reduce_fusion.2
  4.3 0.6 add_select_fusion.1.last_t
  4.9 0.7 constant_dynamic-slice_fusion.2
  5.6 0.0 copy-done
  5.6 0.1 constant_dynamic-slice_fusion
  5.7 0.1 copy.23
  5.8 0.7 fusion.14.w_cols
  6.5 0.1 fusion.5
  6.6 0.7 copy.22.w_rows
  7.3 0.1 copy.17
  7.4 0.1 eq.120
  7.5 0.3 compare_reduce_fusion
  7.8 0.1 and.170
  7.9 1.2 convert_reduce_fusion.1
  9.1 0.6 select_reduce_fusion.2
  9.7 0.1 select_bitcast_fusion
  9.8 0.1 copy.18
  9.9 0.7 reshape.299.send_t
  10.6 0.1 copy.20
  10.6 0.7 reshape.301.take_t
  11.3 0.0 copy-done.1
  11.3 107.0 %gcn_step.1 = (bf16[64,2048]{1,0:T(8,128)(2,1)}, f32[32,256]{1,0:T(8,128)}, f32[32,2048]{1,0:T(8,128)}) custom-call(s32[256]{0:T(256)} %reshape.299.send_t, s32[256]{0:T(256)} %copy-done.1, s32[256]{0:T(256)} %get-tuple-element.6.order_t, f32[256]{0:T(256)} %add_convert_fusion.keep_t, s32[272]{0:T(512)} %add_select_fusion.1.last_t, s32[1024]{0:T(1024)} %reshape.301.take_t, ...), custom_call_target="tpu_custom_call" | custom-call | tf_op jit(solution)/shard_map/gcn_step/pallas_call | solution.py:400
  118.3 1.7 %copy.27 = bf16[64,2048]{1,0:T(8,128)(2,1)} copy(bf16[64,2048]{1,0:T(8,128)(2,1)} %get-tuple-element.12) | data formatting | bytes 524288
  120.0 1.4 %copy.28 = f32[32,256]{1,0:T(8,128)} copy(f32[32,256]{1,0:T(8,128)} %get-tuple-element.13) | data formatting | bytes 65536
  121.4 1.7 %copy.29 = f32[32,2048]{1,0:T(8,128)} copy(f32[32,2048]{1,0:T(8,128)} %get-tuple-element.14) | data formatting | bytes 524288
  (7 shorter events, 0.1 us)
Async XLA Ops:
  0.6 5.0 %copy-start = (bf16[128,256]{1,0:T(8,128)(2,1)S(1)}, bf16[128,256]{1,0:T(8,128)(2,1)}, u32[]{:S(2)}) copy-start(bf16[128,256]{1,0:T(8,128)(2,1)} %param.8) | copy-start | bytes 196612
  2.4 8.9 %copy-start.1 = (s32[256]{0:T(256)}, s32[256]{0:T(256)S(1)}, u32[]{:S(2)}) copy-start(s32[256]{0:T(256)S(1)} %compare_select_fusion.slot_t) | copy-start | bytes 3076

commit v2 on v1

v2 whole, which is shorter than its diff:
```python
import math

import jax
import jax.numpy as jnp
from jax import lax
from jax.experimental import pallas as pl
from jax.experimental.pallas import tpu as pltpu
from jax.sharding import PartitionSpec as P

MESH = pl.DeviceIdType.MESH
NZ, NY, NC, NX = 8, 4, 2, 4
BLK, KB, TILE, CAP, FR, UR = 16, 16, 128, 4, 32, 64
NODES_DEV = BLK * TILE
CH = 4
CN = NODES_DEV // CH
OWN = 64 * CAP
ZERO = BLK * KB
FWD_ORDER = (0, 7, 1, 6, 2, 5, 3, 4)
BWD_ORDER = (4, 3, 5, 2, 6, 1, 7, 0)
FWIN, BWIN, LAG = 2, 2, 3
F32, BF16 = jnp.float32, jnp.bfloat16
NT = (((1,), (1,)), ((), ()))


def group_sum(v, lane):
    n = v.shape[1]
    for step in (1, 2, 4, 8):
        up = pltpu.roll(v, n - step, 1)
        down = pltpu.roll(v, step, 1)
        v = v + jnp.where((lane & step) == 0, up, down)
    return v


def group_rank(named, lane):
    rank = jnp.zeros_like(named)
    for step in range(1, BLK):
        rank = rank + jnp.where((lane & (BLK - 1)) >= step, pltpu.roll(named, step, 1), 0)
    return rank


def send_tables(rows8, send_v, take_v, y, z, c, me):
    lane = lax.broadcasted_iota(jnp.int32, (8 * BLK, TILE), 1)
    target = (lane >> 4) * (8 * BLK) + (lane & 15) + (y * 2 + c) * BLK
    hit = jnp.zeros((8 * BLK, TILE), jnp.int32)
    for k in range(KB):
        hit = jnp.where(rows8[:, k:k + 1] == target, 1, hit)
    named = jnp.max(hit.reshape(8, BLK, TILE), axis=1)
    lane = lax.broadcasted_iota(jnp.int32, (8, TILE), 1)
    rank = group_rank(named, lane)
    for k in range(CAP):
        send_v[k * 8:(k + 1) * 8] = group_sum(jnp.where((named > 0) & (rank == k), lane & 15, 0), lane)
    d = lax.broadcasted_iota(jnp.int32, (8, TILE), 0)
    use = (named > 0) & ((d != me) | ((lane >> 4) != z))
    take_v[...] = jnp.where(use, d * CAP + jnp.minimum(rank, CAP - 1), 8 * CAP)


def slot_tables(rows8, slot_v, prev_v, last_v, r, me):
    own = rows8[pl.ds(pl.multiple_of(me * BLK, BLK), BLK)]
    lane = lax.broadcasted_iota(jnp.int32, (BLK, 64 * BLK), 1)
    hit = jnp.zeros((BLK, 64 * BLK), jnp.int32)
    for k in range(KB):
        hit = jnp.where(own[:, k:k + 1] == lane, 1, hit)
    lane8 = lax.broadcasted_iota(jnp.int32, (8, 64 * BLK), 1)
    named = jnp.broadcast_to(jnp.max(hit, axis=0, keepdims=True), (8, 64 * BLK))
    value = (lane8 >> 4) * CAP + jnp.minimum(group_rank(named, lane8), CAP - 1)
    value = jnp.where((lane8 >> 4) == r, OWN + (lane8 & 15), value)
    value = jnp.concatenate([value, value], axis=0)
    small = lax.broadcasted_iota(jnp.int32, (BLK, TILE), 1)
    e_lane = lax.broadcasted_iota(jnp.int32, (BLK, BLK * KB), 1)
    row = lax.broadcasted_iota(jnp.int32, (BLK, BLK * KB), 0)
    t_lane = lax.broadcasted_iota(jnp.int32, (BLK, 3 * TILE), 1)
    t_row = lax.broadcasted_iota(jnp.int32, (BLK, 3 * TILE), 0)
    slots = jnp.zeros((BLK, TILE), jnp.int32)
    spread = jnp.zeros((BLK, BLK * KB), jnp.int32)
    last = jnp.full((BLK, 3 * TILE), -1, jnp.int32)
    columns = []
    for k in range(KB):
        col = jnp.max(jnp.where(own[:, k:k + 1] == lane, value, 0), axis=1, keepdims=True)
        columns.append(col)
        slots = jnp.where(small == k, col, slots)
        spread = jnp.where((e_lane & 15) == k, col, spread)
        last = jnp.maximum(last, jnp.where(col == t_lane, t_row * KB + k, -1))
    slot_v[...] = slots
    by_lane = jnp.max(jnp.where((e_lane >> 4) == row, spread, 0), axis=0, keepdims=True)
    prev = jnp.zeros((BLK, TILE), jnp.int32)
    for k in range(KB):
        same = (columns[k] == by_lane) & (e_lane < row * KB + k)
        before = jnp.max(jnp.where(same, e_lane, -1), axis=1, keepdims=True)
        prev = jnp.where(small == k, before, prev)
    prev_v[...] = jnp.where(prev < 0, ZERO, prev)
    last = jnp.broadcast_to(jnp.max(last, axis=0, keepdims=True), (8, 3 * TILE))
    last_v[...] = jnp.where(last < 0, ZERO, last)


def kernel(
    feats_hbm, index_hbm, adj_hbm, weight_hbm, cot_hbm,
    out_hbm, wg_hbm, fg_hbm,
    feats, index, rows8, weight, cot, out, wg_out, fg_out,
    send_v, take_v, slot_v, prev_v, last_v, send_t, take_t, slot_t, prev_t, last_t,
    adj, zb, pk, panel, fwp, fwm, xg, gsend, grecv, gown, grad, pref, pk2, rb, fw2p, fw2m, zs_buf, zrp, zrm,
    wpart, wsib, wy, wz, wx, wt,
    lss, zss, zrs, yss, yrs, xss, xrs, gss, grs, yss2, yrs2, zss2, zrs2, wss, wrs,
):
    r = lax.axis_index("rows")
    x = lax.axis_index("cols")
    z, y, c = r // 8, (r // 2) % 4, r % 2
    me = y * 2 + c

    def dev(dz=0, dy=0, dc=0, dx=0):
        row = ((z + dz) % NZ) * 8 + ((y + dy) % NY) * 2 + (c + dc) % 2
        return {"rows": row, "cols": (x + dx) % NX}

    def rcopy(src, dst, ss, rs, **off):
        return pltpu.make_async_remote_copy(
            src_ref=src, dst_ref=dst, send_sem=ss, recv_sem=rs, device_id=dev(**off), device_id_type=MESH
        )

    def local(n, src, dst):
        cp = pltpu.make_async_copy(src, dst, lss.at[n])
        cp.start()
        return cp

    rows_copy = local(0, index_hbm.at[:, pl.ds(pl.multiple_of(z * 8 * BLK, 8 * BLK), 8 * BLK)], index)
    feats_copy = local(1, feats_hbm, feats)
    peers = [dict(dz=d) for d in range(1, 8)]
    peers += [dict(dy=a, dc=b) for a in range(4) for b in range(2) if (a or b) and (a, b) != (2, 1)]
    peers += [dict(dx=a, dc=b) for a in range(1, 4) for b in range(2)]
    barrier = pltpu.get_barrier_semaphore()
    for off in peers:
        pl.semaphore_signal(barrier, inc=1, device_id=dev(**off), device_id_type=MESH)

    weight_copy = local(2, weight_hbm, weight)
    cot_copy = local(3, cot_hbm, cot)
    adj_copy = local(4, adj_hbm, adj)
    rows_copy.wait()
    rows8[...] = index[...].T
    send_tables(rows8, send_v, take_v, y, z, c, me)
    send_copy = local(5, send_v, send_t)
    take_copy = local(6, take_v, take_t)
    feats_copy.wait()
    for b in range(BLK):
        blk = feats[:, b * TILE:(b + 1) * TILE]
        zb[0][b] = blk
        panel[OWN + b] = blk
    pl.semaphore_wait(barrier, len(peers))

    pending = []
    sent = {}
    done = set()

    half = BLK // 2
    whole = pl.ds(0, BLK)
    zcopies = {}

    def zsend(src, dst, direction, blocks):
        cp = rcopy(zb[src].at[blocks], zb[dst].at[blocks], zss.at[dst + 8 * (direction > 0)], zrs.at[dst + 8 * (direction > 0)], dz=direction)
        cp.start()
        zcopies.setdefault(dst, []).append(cp)
        pending.append(cp)

    def pack(dz, src, put, self_put):
        zs = (z + dz) % NZ

        def one(i, carry):
            dd = ((y + i // 2) % NY) * 2 + (c + i % 2) % 2
            src(i, dd, zs)
            return carry

        lax.fori_loop(0 if self_put else 1, 8, one, 0)

    def ysends(dz, packs, dst_of, fp, fm, ss, rs, copies):
        list_ = []
        for n, (dy, dc) in enumerate(((1, 0), (1, 1), (3, 0), (3, 1), (0, 1))):
            cp = rcopy(packs.at[dz, dy * 2 + dc], dst_of(dz, y), ss.at[dz * 9 + n], rs.at[dz * 9 + n], dy=dy, dc=dc)
            list_.append(cp)
        a = rcopy(packs.at[dz, 4], fp.at[dz], ss.at[dz * 9 + 7], rs.at[dz * 9 + 7], dy=1)
        b = rcopy(packs.at[dz, 5], fm.at[dz], ss.at[dz * 9 + 8], rs.at[dz * 9 + 8], dy=3)
        for cp in (a, b, *list_):
            cp.start()
            pending.append(cp)
        copies[dz] = (list_, a, b)
        sent[dz] = (a, b, *list_)

    def throttle(dz):
        for cp in sent[dz]:
            cp.wait_send()
            done.add(id(cp))

    def forwards(dz, dst_of, fp, fm, ss, rs, copies):
        list_, a, b = copies[dz]
        a.wait_recv()
        f = rcopy(fp.at[dz], dst_of(dz, (y + 3) % NY), ss.at[dz * 9 + 5], rs.at[dz * 9 + 5], dy=1, dc=0)
        f.start()
        b.wait_recv()
        g = rcopy(fm.at[dz], dst_of(dz, (y + 1) % NY), ss.at[dz * 9 + 6], rs.at[dz * 9 + 6], dy=3, dc=1)
        g.start()
        pending.extend((f, g))
        list_ += [f, g]

    def panel_of(dz, yy):
        return panel.at[pl.ds((((z + dz) % NZ) * 8 + yy * 2 + c) * CAP, CAP)]

    ycopies = {}
    zsend(0, 7, 1, whole)
    zsend(0, 1, -1, whole)
    send_copy.wait()
    previous = None
    for at, dz in enumerate(FWD_ORDER):
        if dz:
            for cp in zcopies[dz]:
                cp.wait_recv()
            if dz in (7, 6):
                zsend(dz, dz - 1, 1, whole)
            elif dz == 5:
                zsend(5, 4, 1, pl.ds(0, half))
            elif dz in (1, 2):
                zsend(dz, dz + 1, -1, whole)
            elif dz == 3:
                zsend(3, 4, -1, pl.ds(half, half))

        def message(i, dd, zs, dz=dz):
            for k in range(CAP):
                pk[dz, i, k] = zb[dz][send_t[k * 8 + dd, zs * BLK]]

        pack(dz, message, None, False)
        if dz:
            zs = (z + dz) % NZ
            for k in range(CAP):
                panel[(zs * 8 + me) * CAP + k] = zb[dz][send_t[k * 8 + me, zs * BLK]]
        if FWIN and at >= FWIN:
            throttle(FWD_ORDER[at - FWIN])
        ysends(dz, pk, panel_of, fwp, fwm, yss, yrs, ycopies)
        if at == 0:
            slot_tables(rows8, slot_v, prev_v, last_v, r, me)
            table_copies = [local(7, slot_v, slot_t), local(8, prev_v, prev_t), local(9, last_v, last_t)]
        if previous is not None:
            forwards(previous, panel_of, fwp, fwm, yss, yrs, ycopies)
        previous = dz
    forwards(previous, panel_of, fwp, fwm, yss, yrs, ycopies)
    weight_copy.wait()
    w_all = jnp.concatenate(
        [weight[pl.ds(pl.multiple_of(((x + dx) % NX) * FR, FR), FR)] for dx in range(NX)], axis=0
    )
    unit = lax.broadcasted_iota(jnp.int32, (UR, NX * UR), 1) - lax.broadcasted_iota(jnp.int32, (UR, NX * UR), 0)
    pick = jnp.where(unit == x * UR, 1.0, 0.0).astype(BF16)
    w_rows = lax.dot_general(w_all, pick, NT, preferred_element_type=F32).astype(BF16)
    w_cols = lax.dot_general(pick, w_all, NT, preferred_element_type=F32).astype(BF16)
    for cp in (take_copy, *table_copies, cot_copy, adj_copy):
        cp.wait()
    for dz in FWD_ORDER:
        for cp in ycopies[dz][0]:
            cp.wait_recv()

    xcopies = {}
    for q in range(CH):

        def block(n, carry, q=q):
            i = q * (BLK // CH) + n
            acc = jnp.zeros((TILE, FR), F32)
            for k in range(0, KB, 2):
                left = jnp.concatenate([adj[i * KB + k], adj[i * KB + k + 1]], axis=1)
                right = jnp.concatenate([panel[slot_t[i, k]], panel[slot_t[i, k + 1]]], axis=1)
                acc += lax.dot_general(left, right, NT, preferred_element_type=F32)
            xg[0, q, :, pl.ds(pl.multiple_of(n * TILE, TILE), TILE)] = acc.T.astype(BF16)
            return carry

        lax.fori_loop(0, BLK // CH, block, 0)
        for dx in (2, 1, 3):
            cp = rcopy(xg.at[0, q], xg.at[4 - dx, q], xss.at[q * 4 + dx], xrs.at[q * 4 + dx], dx=dx)
            cp.start()
            pending.append(cp)
            xcopies[q, dx] = cp

    gcopies = {}
    out_copies = []
    for q in range(CH):
        cols = pl.ds(q * CN, CN)
        for dx in (1, 3, 2):
            xcopies[q, dx].wait_recv()
        agg = xg[:, q].reshape(NX * FR, CN)
        pre = jnp.dot(w_cols, agg, preferred_element_type=F32)
        sig = jax.nn.sigmoid(pre)
        out[:, cols] = (pre * sig).astype(BF16)
        out_copies.append(local(10 + q, out.at[:, cols], out_hbm.at[:, cols]))
        pg = (cot[:, cols].astype(F32) * sig * (1.0 + pre * (1.0 - sig))).astype(BF16)
        part = jnp.dot(w_rows, pg, preferred_element_type=F32)
        gown[q] = part[0:FR]
        for dx in (2, 1, 3):
            gsend[dx, q] = part[dx * FR:(dx + 1) * FR].astype(BF16)
            cp = rcopy(gsend.at[dx, q], grecv.at[4 - dx, q], gss.at[q * 4 + dx], grs.at[q * 4 + dx], dx=dx)
            cp.start()
            pending.append(cp)
            gcopies[q, dx] = cp
        wg = lax.dot_general(pg, agg, NT, preferred_element_type=F32)
        if q == 0:
            wpart[...] = wg
        else:
            wpart[...] += wg

    hu = UR // 2
    w1 = rcopy(wpart.at[pl.ds(pl.multiple_of((1 - c) * hu, 8), hu)], wsib, wss.at[0], wrs.at[0], dc=1)
    w1.start()
    pending.append(w1)

    for q in range(CH):
        for dx in (1, 3, 2):
            gcopies[q, dx].wait_recv()
        g = gown[q] + grecv[1, q].astype(F32) + grecv[2, q].astype(F32) + grecv[3, q].astype(F32)
        g = g.astype(BF16)
        for n in range(BLK // CH):
            grad[q * (BLK // CH) + n] = g[:, n * TILE:(n + 1) * TILE]

    w1.wait_recv()
    wy[y] = wpart[pl.ds(pl.multiple_of(c * hu, 8), hu)] + wsib[...]
    w2 = []
    for dy in (1, 2, 3):
        cp = rcopy(wy.at[y], wy.at[y], wss.at[dy], wrs.at[dy], dy=dy)
        cp.start()
        pending.append(cp)
        w2.append(cp)

    pref[ZERO] = jnp.zeros((FR, TILE), F32)

    def terms(i, carry):
        g = grad[i]
        for k in range(0, KB, 2):
            e = i * KB + k
            pair = jnp.concatenate([adj[e], adj[e + 1]], axis=1)
            term = jnp.dot(g, pair, preferred_element_type=F32)
            pref[e] = term[:, :TILE] + pref[prev_t[i, k]]
            pref[e + 1] = term[:, TILE:] + pref[prev_t[i, k + 1]]
        return carry

    lax.fori_loop(0, BLK, terms, 0)

    for cp in w2:
        cp.wait_recv()
    wz[z] = (wy[0] + wy[1]) + (wy[2] + wy[3])
    w3 = []
    for dz in range(1, NZ):
        cp = rcopy(wz.at[z], wz.at[z], wss.at[3 + dz], wrs.at[3 + dz], dz=dz)
        cp.start()
        pending.append(cp)
        w3.append(cp)

    ycopies2 = {}

    def rb_of(dz, yy):
        return rb[dz].at[pl.ds((yy * 2 + c) * CAP, CAP)]

    for dz in range(NZ):
        rb[dz][8 * CAP] = jnp.zeros((FR, TILE), BF16)
    zin = {}

    def reduce_chunk(dz):
        for cp in ycopies2[dz][0]:
            cp.wait_recv()
        for cp in zin.get(dz, ()):
            cp.wait_recv()
        zs = (z + dz) % NZ

        def total(b, carry, dz=dz, zs=zs):
            acc = jnp.zeros((FR, TILE), F32)
            for n in range(8):
                acc += rb[dz][take_t[n, zs * BLK + b]].astype(F32)
            if dz in (1, 2):
                acc += zrp[dz, b].astype(F32)
            if dz in (6, 7):
                acc += zrm[dz, b].astype(F32)
            if dz == 0:
                acc += zrp[0, b].astype(F32) + zrm[0, b].astype(F32) + pref[last_t[0, OWN + b]]
                fg_out[:, pl.ds(pl.multiple_of(b * TILE, TILE), TILE)] = acc
            else:
                zs_buf[dz, b] = acc.astype(BF16)
            return carry

        def total_more(b, carry, dz=dz, zs=zs):
            off = 0 if dz == 3 else half
            acc = (zrp if dz == 3 else zrm)[dz, off + b].astype(F32)
            for n in range(8):
                acc += rb[dz][take_t[n, zs * BLK + off + b]].astype(F32)
            zs_buf[dz, off + b] = acc.astype(BF16)
            return carry

        def total_less(b, carry, dz=dz, zs=zs):
            off = half if dz == 3 else 0
            acc = jnp.zeros((FR, TILE), F32)
            for n in range(8):
                acc += rb[dz][take_t[n, zs * BLK + off + b]].astype(F32)
            zs_buf[dz, off + b] = acc.astype(BF16)
            return carry

        if dz in (3, 5):
            lax.fori_loop(0, half, total_more, 0)
            lax.fori_loop(0, half, total_less, 0)
        else:
            lax.fori_loop(0, BLK, total, 0)

        def ring(direction, blocks):
            to = dz - direction if dz - direction != 8 else 0
            buf = zrp if direction > 0 else zrm
            n = dz + 8 * (direction > 0)
            cp = rcopy(zs_buf.at[dz, blocks], buf.at[to, blocks], zss2.at[n], zrs2.at[n], dz=direction)
            cp.start()
            pending.append(cp)
            zin.setdefault(to, []).append(cp)

        if dz == 4:
            ring(1, pl.ds(0, half))
            ring(-1, pl.ds(half, half))
        elif dz in (1, 2, 3):
            ring(1, whole)
        elif dz in (5, 6, 7):
            ring(-1, whole)

    def weight_cols():
        for cp in w3:
            cp.wait_recv()
        wx[0, c] = (((wz[0] + wz[1]) + (wz[2] + wz[3])) + ((wz[4] + wz[5]) + (wz[6] + wz[7]))) * (
            1.0 / math.sqrt(NODES_DEV * 64)
        )
        w4 = []
        for dx in range(4):
            for dc in range(2):
                if dx or dc:
                    n = 11 + dx * 2 + dc
                    cp = rcopy(wx.at[0, c], wx.at[(4 - dx) % 4, c], wss.at[n], wrs.at[n], dx=dx, dc=dc)
                    cp.start()
                    pending.append(cp)
                    w4.append(cp)
        return w4

    sent.clear()
    for at, dz in enumerate(BWD_ORDER):

        def term(i, dd, zs, dz=dz):
            for k in range(CAP):
                pk2[dz, i, k] = pref[last_t[0, (zs * 8 + dd) * CAP + k]].astype(BF16)

        pack(dz, term, None, False)
        zs = (z + dz) % NZ
        for k in range(CAP):
            if dz:
                rb[dz][me * CAP + k] = pref[last_t[0, (zs * 8 + me) * CAP + k]].astype(BF16)
            else:
                rb[dz][me * CAP + k] = jnp.zeros((FR, TILE), BF16)
        if BWIN and at >= BWIN:
            throttle(BWD_ORDER[at - BWIN])
        ysends(dz, pk2, rb_of, fw2p, fw2m, yss2, yrs2, ycopies2)
        if at:
            forwards(BWD_ORDER[at - 1], rb_of, fw2p, fw2m, yss2, yrs2, ycopies2)
        if at == 3:
            w4 = weight_cols()
        if at >= LAG:
            reduce_chunk(BWD_ORDER[at - LAG])
    forwards(0, rb_of, fw2p, fw2m, yss2, yrs2, ycopies2)
    for dz in BWD_ORDER[NZ - LAG:]:
        reduce_chunk(dz)

    for cp in w4:
        cp.wait_recv()
    for dx in range(4):
        for cc in range(2):
            f0 = ((4 - dx) % 4) * FR
            row = pl.multiple_of(((x + dx) % NX) * UR + cc * hu, 8)
            wt[pl.ds(row, hu), 0:FR] = wx[dx, cc][:, f0:f0 + FR]
    wg_out[...] = wt[...].T[0:FR]
    out_copies += [local(14, wg_out, wg_hbm), local(15, fg_out, fg_hbm)]
    for cp in out_copies:
        cp.wait()

    for cp in pending:
        if id(cp) not in done:
            cp.wait_send()


def keep(a, b, c, a_out, b_out, c_out):
    a_out[...] = a[...]
    b_out[...] = b[...]
    c_out[...] = c[...]


def body(feats_t, adj_index, adj_weight, weight, cotangent_t):
    hbm = pl.BlockSpec(memory_space=pl.ANY)
    dma = pltpu.SemaphoreType.DMA
    blk = (FR, TILE)
    V = pltpu.VMEM
    table = lambda space: [space(s, jnp.int32) for s in ((4 * 8, TILE), (8, TILE), (BLK, TILE), (BLK, TILE), (8, 3 * TILE))]
    shapes = (
        jax.ShapeDtypeStruct((UR, NODES_DEV), BF16),
        jax.ShapeDtypeStruct((FR, NX * UR), F32),
        jax.ShapeDtypeStruct((FR, NODES_DEV), F32),
    )
    outs = pl.pallas_call(
        kernel,
        out_shape=shapes,
        in_specs=[hbm] * 5,
        out_specs=(hbm,) * 3,
        scratch_shapes=[
            V((FR, NODES_DEV), BF16),
            V((KB, 8 * BLK), jnp.int32),
            V((8 * BLK, KB), jnp.int32),
            V((NX * FR, NX * UR), BF16),
            V((UR, NODES_DEV), BF16),
            V((UR, NODES_DEV), BF16),
            V((FR, NX * UR), F32),
            V((FR, NODES_DEV), F32),
            *table(V),
            *table(pltpu.SMEM),
            V((BLK * KB, TILE, TILE), BF16),
            [V((BLK, *blk), BF16) for _ in range(NZ)],
            V((NZ, 8, CAP, *blk), BF16),
            V((OWN + BLK, *blk), BF16),
            V((NZ, CAP, *blk), BF16),
            V((NZ, CAP, *blk), BF16),
            V((NX, CH, FR, CN), BF16),
            V((NX, CH, FR, CN), BF16),
            V((NX, CH, FR, CN), BF16),
            V((CH, FR, CN), F32),
            V((BLK, *blk), BF16),
            V((BLK * KB + 1, *blk), F32),
            V((NZ, 8, CAP, *blk), BF16),
            [V((8 * CAP + 1, *blk), BF16) for _ in range(NZ)],
            V((NZ, CAP, *blk), BF16),
            V((NZ, CAP, *blk), BF16),
            V((NZ, BLK, *blk), BF16),
            V((NZ, BLK, *blk), BF16),
            V((NZ, BLK, *blk), BF16),
            V((UR, NX * FR), F32),
            V((UR // 2, NX * FR), F32),
            V((NY, UR // 2, NX * FR), F32),
            V((NZ, UR // 2, NX * FR), F32),
            V((NX, NC, UR // 2, NX * FR), F32),
            V((NX * UR, TILE), F32),
            dma((16,)),
            dma((16,)),
            dma((16,)),
            dma((9 * NZ,)),
            dma((9 * NZ,)),
            dma((16,)),
            dma((16,)),
            dma((16,)),
            dma((16,)),
            dma((9 * NZ,)),
            dma((9 * NZ,)),
            dma((16,)),
            dma((16,)),
            dma((19,)),
            dma((19,)),
        ],
        compiler_params=pltpu.CompilerParams(
            collective_id=0, has_side_effects=True, vmem_limit_bytes=56 * 2**20
        ),
        name="gcn_step",
    )(feats_t, adj_index.T, adj_weight.reshape(BLK * KB, TILE, TILE), weight, cotangent_t)
    return pl.pallas_call(
        keep,
        out_shape=shapes,
        name="results",
    )(*outs)


def solution(mesh):
    return jax.shard_map(
        body,
        mesh=mesh,
        in_specs=(P("cols", "rows"), P(), P("rows", None, None, None), P(), P("cols", "rows")),
        out_specs=(P("cols", "rows"), P("cols", None), P("cols", "rows")),
        check_vma=False,
    )
```

time: 123 us -> 92.8 us (0.75)
  Pallas kernels: 107 us -> 91.6 us
  local copies, waits for them, and re-layouts: 9.06 us -> 0 us
  other arithmetic: 6.2 us -> 0 us
    pallas_call x1 -> x2, Pallas kernels: 107 us -> 91.6 us  [the longest x1 89.7 us: body(): pl.pallas_call(kernel, out_shape=shapes, in_specs=[hbm] * 5, out_specs=(h...]
    unnamed x8 -> x0, local copies, waits for them, and re-layouts: 4.81 us -> none
    reduce_sum x6 -> x0, other arithmetic: 3.33 us -> none  [the longest x1 1.16 us: tables(): jnp.sum(jnp.where((b[None, :] < b[:, None])[None, None], named[:, :, None...]
    dynamic_slice x6 -> x0, local copies, waits for them, and re-layouts: 2.45 us -> none  [the longest x2 0.85 us: tables(): own = lax.dynamic_slice_in_dim(adj_index, r * BLK, BLK, 0).reshape(BLK * KB)]
    reshape x3 -> x0, local copies, waits for them, and re-layouts: 1.43 us -> none  [the longest x2 1.34 us: tables(): return (send.reshape(-1), slot, order, keep, last, take.reshape(-1))]
where the time goes in v2:
time: 92.8 us; the launch traced here: 92.2 us
  Pallas kernels  91.6 us (99%)
    pallas_call x1, Pallas kernels, body(): pl.pallas_call(kernel, out_shape=shapes, in_specs=[hbm] * 5, out_specs=(h...  89.7 us
    pallas_call x1, Pallas kernels, body(): return pl.pallas_call(keep, out_shape=shapes, name='results')(*outs)  1.86 us

profile of v2, /device:TPU:8, one launch (start us, length us, event | category | flops | bytes accessed | tf_op | source)
XLA Modules:
  0.0 92.2 jit_solution(8258978266427960072)
XLA Ops:
  0.6 89.7 %gcn_step.1 = (bf16[64,2048]{1,0:T(8,128)(2,1)}, f32[32,256]{1,0:T(8,128)}, f32[32,2048]{1,0:T(8,128)}) custom-call(bf16[32,2048]{1,0:T(8,128)(2,1)} %feats_hbm.1, s32[16,1024]{1,0:T(8,128)} %bitcast.3, bf16[256,128,128]{2,1,0:T(8,128)(2,1)} %bitcast.2, bf16[128,256]{1,0:T(8,128)(2,1)} %weight_hbm.1, bf16[64,2048]{1,0:T(8,128)(2,1)} %cot_hbm.1), custom_call_target="tpu_custom_call" | custom-call | tf_op jit(solution)/shard_map/gcn_step/pallas_call | solution.py:494
  90.3 1.9 %results.1 = (bf16[64,2048]{1,0:T(8,128)(2,1)}, f32[32,256]{1,0:T(8,128)}, f32[32,2048]{1,0:T(8,128)}) custom-call(bf16[64,2048]{1,0:T(8,128)(2,1)} %get-tuple-element.6.a, f32[32,256]{1,0:T(8,128)} %get-tuple-element.7.b, f32[32,2048]{1,0:T(8,128)} %get-tuple-element.8.c), custom_call_target="tpu_custom_call" | custom-call | tf_op jit(solution)/shard_map/results/pallas_call | solution.py:556

commit v3 on v2

--- a/solution.py
+++ b/solution.py
@@ -302,23 +302,6 @@
     w1.start()
     pending.append(w1)
 
-    for q in range(CH):
-        for dx in (1, 3, 2):
-            gcopies[q, dx].wait_recv()
-        g = gown[q] + grecv[1, q].astype(F32) + grecv[2, q].astype(F32) + grecv[3, q].astype(F32)
-        g = g.astype(BF16)
-        for n in range(BLK // CH):
-            grad[q * (BLK // CH) + n] = g[:, n * TILE:(n + 1) * TILE]
-
-    w1.wait_recv()
-    wy[y] = wpart[pl.ds(pl.multiple_of(c * hu, 8), hu)] + wsib[...]
-    w2 = []
-    for dy in (1, 2, 3):
-        cp = rcopy(wy.at[y], wy.at[y], wss.at[dy], wrs.at[dy], dy=dy)
-        cp.start()
-        pending.append(cp)
-        w2.append(cp)
-
     pref[ZERO] = jnp.zeros((FR, TILE), F32)
 
     def terms(i, carry):
@@ -331,7 +314,25 @@
             pref[e + 1] = term[:, TILE:] + pref[prev_t[i, k + 1]]
         return carry
 
-    lax.fori_loop(0, BLK, terms, 0)
+    nb = BLK // CH
+    for q in range(CH):
+        for dx in (1, 3, 2):
+            gcopies[q, dx].wait_recv()
+        g = gown[q] + grecv[1, q].astype(F32) + grecv[2, q].astype(F32) + grecv[3, q].astype(F32)
+        g = g.astype(BF16)
+        for n in range(nb):
+            grad[q * nb + n] = g[:, n * TILE:(n + 1) * TILE]
+        lax.fori_loop(q * nb, (q + 1) * nb, terms, 0)
+        if q == 1:
+            w1.wait_recv()
+            wy[y] = wpart[pl.ds(pl.multiple_of(c * hu, 8), hu)] + wsib[...]
+            w2 = []
+            for dy in (1, 2, 3):
+                cp = rcopy(wy.at[y], wy.at[y], wss.at[dy], wrs.at[dy], dy=dy)
+                cp.start()
+                pending.append(cp)
+                w2.append(cp)
+
 
     for cp in w2:
         cp.wait_recv()
@@ -355,63 +356,38 @@
     def reduce_chunk(dz):
         for cp in ycopies2[dz][0]:
             cp.wait_recv()
-        for cp in zin.get(dz, ()):
-            cp.wait_recv()
         zs = (z + dz) % NZ
-
-        def total(b, carry, dz=dz, zs=zs):
-            acc = jnp.zeros((FR, TILE), F32)
-            for n in range(8):
-                acc += rb[dz][take_t[n, zs * BLK + b]].astype(F32)
-            if dz in (1, 2):
-                acc += zrp[dz, b].astype(F32)
-            if dz in (6, 7):
-                acc += zrm[dz, b].astype(F32)
-            if dz == 0:
-                acc += zrp[0, b].astype(F32) + zrm[0, b].astype(F32) + pref[last_t[0, OWN + b]]
-                fg_out[:, pl.ds(pl.multiple_of(b * TILE, TILE), TILE)] = acc
-            else:
-                zs_buf[dz, b] = acc.astype(BF16)
-            return carry
-
-        def total_more(b, carry, dz=dz, zs=zs):
-            off = 0 if dz == 3 else half
-            acc = (zrp if dz == 3 else zrm)[dz, off + b].astype(F32)
-            for n in range(8):
-                acc += rb[dz][take_t[n, zs * BLK + off + b]].astype(F32)
-            zs_buf[dz, off + b] = acc.astype(BF16)
-            return carry
-
-        def total_less(b, carry, dz=dz, zs=zs):
-            off = half if dz == 3 else 0
-            acc = jnp.zeros((FR, TILE), F32)
-            for n in range(8):
-                acc += rb[dz][take_t[n, zs * BLK + off + b]].astype(F32)
-            zs_buf[dz, off + b] = acc.astype(BF16)
-            return carry
-
-        if dz in (3, 5):
-            lax.fori_loop(0, half, total_more, 0)
-            lax.fori_loop(0, half, total_less, 0)
-        else:
-            lax.fori_loop(0, BLK, total, 0)
-
-        def ring(direction, blocks):
-            to = dz - direction if dz - direction != 8 else 0
-            buf = zrp if direction > 0 else zrm
-            n = dz + 8 * (direction > 0)
-            cp = rcopy(zs_buf.at[dz, blocks], buf.at[to, blocks], zss2.at[n], zrs2.at[n], dz=direction)
-            cp.start()
-            pending.append(cp)
-            zin.setdefault(to, []).append(cp)
-
-        if dz == 4:
-            ring(1, pl.ds(0, half))
-            ring(-1, pl.ds(half, half))
-        elif dz in (1, 2, 3):
-            ring(1, whole)
-        elif dz in (5, 6, 7):
-            ring(-1, whole)
+        for h in ((1, 0) if dz == 3 else (0, 1)):
+            arrived = []
+            for cp, buf in zin.get((dz, h), ()):
+                cp.wait_recv()
+                arrived.append(buf)
+
+            def total(n, carry, h=h, arrived=tuple(arrived)):
+                b = h * half + n
+                acc = jnp.zeros((FR, TILE), F32)
+                for d in range(8):
+                    acc += rb[dz][take_t[d, zs * BLK + b]].astype(F32)
+                for buf in arrived:
+                    acc += buf[dz, b].astype(F32)
+                if dz:
+                    zs_buf[dz, b] = acc.astype(BF16)
+                else:
+                    acc += pref[last_t[0, OWN + b]]
+                    fg_out[:, pl.ds(pl.multiple_of(b * TILE, TILE), TILE)] = acc
+                return carry
+
+            lax.fori_loop(0, half, total, 0)
+            if dz:
+                up = dz < 4 or (dz == 4 and h == 0)
+                to = dz - 1 if up else (dz + 1) % NZ
+                buf = zrp if up else zrm
+                blocks = pl.ds(h * half, half)
+                n = dz * 2 + h
+                cp = rcopy(zs_buf.at[dz, blocks], buf.at[to, blocks], zss2.at[n], zrs2.at[n], dz=1 if up else -1)
+                cp.start()
+                pending.append(cp)
+                zin.setdefault((to, h), []).append((cp, buf))
 
     def weight_cols():
         for cp in w3:

time: 92.8 us -> 90.5 us (0.975)
  Pallas kernels: 91.6 us -> 89.1 us
    pallas_call x1, Pallas kernels: 89.7 us -> 87.2 us  [body(): pl.pallas_call(kernel, out_shape=shapes, in_specs=[hbm] * 5, out_specs=(h...]
where the time goes in v3:
time: 90.5 us; the launch traced here: 89.7 us
  Pallas kernels  89.1 us (98%)
    pallas_call x1, Pallas kernels, body(): pl.pallas_call(kernel, out_shape=shapes, in_specs=[hbm] * 5, out_specs=(h...  87.2 us
    pallas_call x1, Pallas kernels, body(): return pl.pallas_call(keep, out_shape=shapes, name='results')(*outs)  1.86 us

profile of v3, /device:TPU:8, one launch (start us, length us, event | category | flops | bytes accessed | tf_op | source)
XLA Modules:
  0.0 89.7 jit_solution(10202192078707071949)
XLA Ops:
  0.6 87.2 %gcn_step.1 = (bf16[64,2048]{1,0:T(8,128)(2,1)}, f32[32,256]{1,0:T(8,128)}, f32[32,2048]{1,0:T(8,128)}) custom-call(bf16[32,2048]{1,0:T(8,128)(2,1)} %feats_hbm.1, s32[16,1024]{1,0:T(8,128)} %bitcast.3, bf16[256,128,128]{2,1,0:T(8,128)(2,1)} %bitcast.2, bf16[128,256]{1,0:T(8,128)(2,1)} %weight_hbm.1, bf16[64,2048]{1,0:T(8,128)(2,1)} %cot_hbm.1), custom_call_target="tpu_custom_call" | custom-call | tf_op jit(solution)/shard_map/gcn_step/pallas_call | solution.py:470
  87.9 1.9 %results.1 = (bf16[64,2048]{1,0:T(8,128)(2,1)}, f32[32,256]{1,0:T(8,128)}, f32[32,2048]{1,0:T(8,128)}) custom-call(bf16[64,2048]{1,0:T(8,128)(2,1)} %get-tuple-element.6.a, f32[32,256]{1,0:T(8,128)} %get-tuple-element.7.b, f32[32,2048]{1,0:T(8,128)} %get-tuple-element.8.c), custom_call_target="tpu_custom_call" | custom-call | tf_op jit(solution)/shard_map/results/pallas_call | solution.py:532

commit v4 on v3

--- a/solution.py
+++ b/solution.py
@@ -17,7 +17,8 @@
 ZERO = BLK * KB
 FWD_ORDER = (0, 7, 1, 6, 2, 5, 3, 4)
 BWD_ORDER = (4, 3, 5, 2, 6, 1, 7, 0)
-FWIN, BWIN, LAG = 2, 2, 3
+LAG = 3
+WAT = (0, 2, 5)
 F32, BF16 = jnp.float32, jnp.bfloat16
 NT = (((1,), (1,)), ((), ()))
 
@@ -168,23 +169,31 @@
 
         lax.fori_loop(0 if self_put else 1, 8, one, 0)
 
-    def ysends(dz, packs, dst_of, fp, fm, ss, rs, copies):
-        list_ = []
+    def first_hops(dz, packs, fp, fm, ss, rs, copies):
+        a = rcopy(packs.at[dz, 4], fp.at[dz], ss.at[dz * 9 + 7], rs.at[dz * 9 + 7], dy=1)
+        b = rcopy(packs.at[dz, 5], fm.at[dz], ss.at[dz * 9 + 8], rs.at[dz * 9 + 8], dy=3)
+        for cp in (a, b):
+            cp.start()
+            pending.append(cp)
+        copies[dz] = ([], a, b)
+
+    def ysends(dz, packs, dst_of, ss, rs, copies):
+        list_, a, b = copies[dz]
         for n, (dy, dc) in enumerate(((1, 0), (1, 1), (3, 0), (3, 1), (0, 1))):
             cp = rcopy(packs.at[dz, dy * 2 + dc], dst_of(dz, y), ss.at[dz * 9 + n], rs.at[dz * 9 + n], dy=dy, dc=dc)
-            list_.append(cp)
-        a = rcopy(packs.at[dz, 4], fp.at[dz], ss.at[dz * 9 + 7], rs.at[dz * 9 + 7], dy=1)
-        b = rcopy(packs.at[dz, 5], fm.at[dz], ss.at[dz * 9 + 8], rs.at[dz * 9 + 8], dy=3)
-        for cp in (a, b, *list_):
             cp.start()
             pending.append(cp)
-        copies[dz] = (list_, a, b)
+            list_.append(cp)
         sent[dz] = (a, b, *list_)
 
+    def drain(copies):
+        for cp in copies:
+            if id(cp) not in done:
+                cp.wait_send()
+                done.add(id(cp))
+
     def throttle(dz):
-        for cp in sent[dz]:
-            cp.wait_send()
-            done.add(id(cp))
+        drain(sent[dz])
 
     def forwards(dz, dst_of, fp, fm, ss, rs, copies):
         list_, a, b = copies[dz]
@@ -204,7 +213,6 @@
     zsend(0, 7, 1, whole)
     zsend(0, 1, -1, whole)
     send_copy.wait()
-    previous = None
     for at, dz in enumerate(FWD_ORDER):
         if dz:
             for cp in zcopies[dz]:
@@ -227,16 +235,19 @@
             zs = (z + dz) % NZ
             for k in range(CAP):
                 panel[(zs * 8 + me) * CAP + k] = zb[dz][send_t[k * 8 + me, zs * BLK]]
-        if FWIN and at >= FWIN:
-            throttle(FWD_ORDER[at - FWIN])
-        ysends(dz, pk, panel_of, fwp, fwm, yss, yrs, ycopies)
+        if at >= 2:
+            throttle(FWD_ORDER[at - 2])
+        first_hops(dz, pk, fwp, fwm, yss, yrs, ycopies)
+        if at:
+            forwards(FWD_ORDER[at - 1], panel_of, fwp, fwm, yss, yrs, ycopies)
+        ysends(dz, pk, panel_of, yss, yrs, ycopies)
         if at == 0:
             slot_tables(rows8, slot_v, prev_v, last_v, r, me)
             table_copies = [local(7, slot_v, slot_t), local(8, prev_v, prev_t), local(9, last_v, last_t)]
-        if previous is not None:
-            forwards(previous, panel_of, fwp, fwm, yss, yrs, ycopies)
-        previous = dz
-    forwards(previous, panel_of, fwp, fwm, yss, yrs, ycopies)
+        if at >= 3:
+            for cp in ycopies[FWD_ORDER[at - 3]][0]:
+                cp.wait_recv()
+    forwards(FWD_ORDER[-1], panel_of, fwp, fwm, yss, yrs, ycopies)
     weight_copy.wait()
     w_all = jnp.concatenate(
         [weight[pl.ds(pl.multiple_of(((x + dx) % NX) * FR, FR), FR)] for dx in range(NX)], axis=0
@@ -247,7 +258,7 @@
     w_cols = lax.dot_general(pick, w_all, NT, preferred_element_type=F32).astype(BF16)
     for cp in (take_copy, *table_copies, cot_copy, adj_copy):
         cp.wait()
-    for dz in FWD_ORDER:
+    for dz in FWD_ORDER[NZ - 3:]:
         for cp in ycopies[dz][0]:
             cp.wait_recv()
 
@@ -264,7 +275,7 @@
             xg[0, q, :, pl.ds(pl.multiple_of(n * TILE, TILE), TILE)] = acc.T.astype(BF16)
             return carry
 
-        lax.fori_loop(0, BLK // CH, block, 0)
+        lax.fori_loop(0, BLK // CH, block, 0, unroll=True)
         for dx in (2, 1, 3):
             cp = rcopy(xg.at[0, q], xg.at[4 - dx, q], xss.at[q * 4 + dx], xrs.at[q * 4 + dx], dx=dx)
             cp.start()
@@ -322,27 +333,30 @@
         g = g.astype(BF16)
         for n in range(nb):
             grad[q * nb + n] = g[:, n * TILE:(n + 1) * TILE]
-        lax.fori_loop(q * nb, (q + 1) * nb, terms, 0)
-        if q == 1:
-            w1.wait_recv()
-            wy[y] = wpart[pl.ds(pl.multiple_of(c * hu, 8), hu)] + wsib[...]
-            w2 = []
-            for dy in (1, 2, 3):
-                cp = rcopy(wy.at[y], wy.at[y], wss.at[dy], wrs.at[dy], dy=dy)
-                cp.start()
-                pending.append(cp)
-                w2.append(cp)
-
-
-    for cp in w2:
-        cp.wait_recv()
-    wz[z] = (wy[0] + wy[1]) + (wy[2] + wy[3])
-    w3 = []
-    for dz in range(1, NZ):
-        cp = rcopy(wz.at[z], wz.at[z], wss.at[3 + dz], wrs.at[3 + dz], dz=dz)
-        cp.start()
-        pending.append(cp)
-        w3.append(cp)
+        lax.fori_loop(q * nb, (q + 1) * nb, terms, 0, unroll=True)
+
+    def weight_y():
+        w1.wait_recv()
+        wy[y] = wpart[pl.ds(pl.multiple_of(c * hu, 8), hu)] + wsib[...]
+        copies = []
+        for dy in (1, 2, 3):
+            cp = rcopy(wy.at[y], wy.at[y], wss.at[dy], wrs.at[dy], dy=dy)
+            cp.start()
+            pending.append(cp)
+            copies.append(cp)
+        return copies
+
+    def weight_z():
+        for cp in w2:
+            cp.wait_recv()
+        wz[z] = (wy[0] + wy[1]) + (wy[2] + wy[3])
+        copies = []
+        for dz in range(1, NZ):
+            cp = rcopy(wz.at[z], wz.at[z], wss.at[3 + dz], wrs.at[3 + dz], dz=dz)
+            cp.start()
+            pending.append(cp)
+            copies.append(cp)
+        return copies
 
     ycopies2 = {}
 
@@ -378,6 +392,9 @@
                 return carry
 
             lax.fori_loop(0, half, total, 0)
+            if not dz:
+                cols = pl.ds(h * half * TILE, half * TILE)
+                out_copies.append(local(15 if h else 9, fg_out.at[:, cols], fg_hbm.at[:, cols]))
             if dz:
                 up = dz < 4 or (dz == 4 and h == 0)
                 to = dz - 1 if up else (dz + 1) % NZ
@@ -407,6 +424,8 @@
         return w4
 
     sent.clear()
+    old = len(pending)
+    marks = []
     for at, dz in enumerate(BWD_ORDER):
 
         def term(i, dd, zs, dz=dz):
@@ -420,17 +439,28 @@
                 rb[dz][me * CAP + k] = pref[last_t[0, (zs * 8 + me) * CAP + k]].astype(BF16)
             else:
                 rb[dz][me * CAP + k] = jnp.zeros((FR, TILE), BF16)
-        if BWIN and at >= BWIN:
-            throttle(BWD_ORDER[at - BWIN])
-        ysends(dz, pk2, rb_of, fw2p, fw2m, yss2, yrs2, ycopies2)
+        if at >= 2:
+            throttle(BWD_ORDER[at - 2])
+        first_hops(dz, pk2, fw2p, fw2m, yss2, yrs2, ycopies2)
         if at:
             forwards(BWD_ORDER[at - 1], rb_of, fw2p, fw2m, yss2, yrs2, ycopies2)
-        if at == 3:
+        ysends(dz, pk2, rb_of, yss2, yrs2, ycopies2)
+        if at == WAT[0]:
+            w2 = weight_y()
+        if at == WAT[1]:
+            w3 = weight_z()
+        if at == WAT[2]:
             w4 = weight_cols()
         if at >= LAG:
             reduce_chunk(BWD_ORDER[at - LAG])
+        marks.append(len(pending))
+        if at < 4:
+            drain(pending[old * at // 4:old * (at + 1) // 4])
+        else:
+            drain(pending[marks[at - 4]:marks[at - 3]])
     forwards(0, rb_of, fw2p, fw2m, yss2, yrs2, ycopies2)
-    for dz in BWD_ORDER[NZ - LAG:]:
+    drain(pending[old:marks[-3]])
+    for dz in BWD_ORDER[NZ - LAG:-1]:
         reduce_chunk(dz)
 
     for cp in w4:
@@ -441,13 +471,13 @@
             row = pl.multiple_of(((x + dx) % NX) * UR + cc * hu, 8)
             wt[pl.ds(row, hu), 0:FR] = wx[dx, cc][:, f0:f0 + FR]
     wg_out[...] = wt[...].T[0:FR]
-    out_copies += [local(14, wg_out, wg_hbm), local(15, fg_out, fg_hbm)]
+    out_copies.append(local(14, wg_out, wg_hbm))
+    drain(pending[:-4])
+    reduce_chunk(0)
     for cp in out_copies:
         cp.wait()
 
-    for cp in pending:
-        if id(cp) not in done:
-            cp.wait_send()
+    drain(pending)
 
 
 def keep(a, b, c, a_out, b_out, c_out):

time: 90.5 us -> 87.7 us (0.969)
  Pallas kernels: 89.1 us -> 86.9 us
    pallas_call x1, Pallas kernels: 87.2 us -> 85 us  [body(): pl.pallas_call(kernel, out_shape=shapes, in_specs=[hbm] * 5, out_specs=(h...]
where the time goes in v4:
time: 87.7 us; the launch traced here: 87.5 us
  Pallas kernels  86.9 us (99%)
    pallas_call x1, Pallas kernels, body(): pl.pallas_call(kernel, out_shape=shapes, in_specs=[hbm] * 5, out_specs=(h...  85 us
    pallas_call x1, Pallas kernels, body(): return pl.pallas_call(keep, out_shape=shapes, name='results')(*outs)  1.86 us

profile of v4, /device:TPU:8, one launch (start us, length us, event | category | flops | bytes accessed | tf_op | source)
XLA Modules:
  0.0 87.5 jit_solution(4396129486469031317)
XLA Ops:
  0.6 85.0 %gcn_step.1 = (bf16[64,2048]{1,0:T(8,128)(2,1)}, f32[32,256]{1,0:T(8,128)}, f32[32,2048]{1,0:T(8,128)}) custom-call(bf16[32,2048]{1,0:T(8,128)(2,1)} %feats_hbm.1, s32[16,1024]{1,0:T(8,128)} %bitcast.3, bf16[256,128,128]{2,1,0:T(8,128)(2,1)} %bitcast.2, bf16[128,256]{1,0:T(8,128)(2,1)} %weight_hbm.1, bf16[64,2048]{1,0:T(8,128)(2,1)} %cot_hbm.1), custom_call_target="tpu_custom_call" | custom-call | tf_op jit(solution)/shard_map/gcn_step/pallas_call | solution.py:500
  85.7 1.9 %results.1 = (bf16[64,2048]{1,0:T(8,128)(2,1)}, f32[32,256]{1,0:T(8,128)}, f32[32,2048]{1,0:T(8,128)}) custom-call(bf16[64,2048]{1,0:T(8,128)(2,1)} %get-tuple-element.6.a, f32[32,256]{1,0:T(8,128)} %get-tuple-element.7.b, f32[32,2048]{1,0:T(8,128)} %get-tuple-element.8.c), custom_call_target="tpu_custom_call" | custom-call | tf_op jit(solution)/shard_map/results/pallas_call | solution.py:562
